TPU v7x, 32 devices: a whole 2x2x4 slice. The times are simulated.
32 devices in a mesh: dx: 4 (over y, x), dy: 8 (over z, core).
Axes of the slice: x: 2, y: 2, z: 4, core: 2. Of those that a mesh axis runs over, the one named last changes fastest.
Arguments:
- audio: bfloat16 [8, 32, 2570], P('dy', 'dx'), may hold values from -6 to 6
- counts: int32 [8, 4], P('dy', 'dx'), may hold values from 1 to 8, 16 in all within a row
- cotangent: bfloat16 [8, 16, 256, 512], P('dy', 'dx'), may hold values from -6 to 6
- conv_first: bfloat16 [10, 512], replicated, may hold values from -2 to 2
- norm_gain: float32 [512], replicated, may hold values from 0.1 to 1.9
- norm_bias: float32 [512], replicated, may hold values from -3 to 3
- conv_second: bfloat16 [1536, 512], replicated, may hold values from -0.15625 to 0.15625
Outputs:
- grad_conv_first: float32 [10, 512], replicated
- grad_norm: float32 [2, 512], replicated
- grad_conv_second: float32 [1536, 512], P('dy')
Inputs may be any that keep to these rules, and one draw needn't show every extreme that they name: In each group along dy the counts sum to 16, and some device of each group holds exactly 8 live crops.
All inputs are finite; a program needn't handle non-finite values.
Results may differ from a plain program's by a relative error of at most 0.0051.
Values may be sent and summed in bfloat16 or wider, within the bound.
No kernel may reach another device: no remote copies, remote signals or barrier semaphores. Data moves between devices by JAX's collectives and lax.ppermute only.
A program may use at most 128 MiB of HBM per device.

v0:
```python
import math

import jax
import jax.numpy as jnp
from jax import lax
from jax.sharding import PartitionSpec as P


def gelu_cdf(value):
    return 0.5 * (1.0 + lax.erf(value * 0.7071067811865476))


def gelu_slope(value):
    return gelu_cdf(value) + value * jnp.exp(-0.5 * value * value) * 0.3989422804014327


def forward_backward(
    crop_waves, cot_rows, conv_first, norm_gain, norm_bias, conv_second, loss_scale
):
    batch_size = crop_waves.shape[0]
    frames = cot_rows.shape[1]
    first_len = 2 * frames + 1
    channels = conv_second.shape[1]
    early_taps = crop_waves[:, : 5 * first_len].reshape(batch_size, first_len, 5)
    late_taps = crop_waves[:, 5 : 5 * first_len + 5].reshape(batch_size, first_len, 5)
    patches = jnp.concatenate([early_taps, late_taps], axis=2).reshape(batch_size * first_len, 10)
    pre_norm = jnp.dot(patches, conv_first, preferred_element_type=jnp.float32).reshape(
        batch_size, first_len, channels
    )
    centre = pre_norm - jnp.mean(pre_norm, axis=1, keepdims=True)
    inv_std = lax.rsqrt(jnp.mean(centre * centre, axis=1, keepdims=True) + 1e-05)
    normed = centre * inv_std
    shifted = normed * norm_gain + norm_bias
    hidden = (shifted * gelu_cdf(shifted)).astype(jnp.bfloat16)
    two_taps = hidden[:, : 2 * frames].reshape(batch_size, frames, 2 * channels)
    third_tap = hidden[:, 2::2]
    second_rows = jnp.concatenate([two_taps, third_tap], axis=2).reshape(
        batch_size * frames, 3 * channels
    )
    pre_act = jnp.dot(second_rows, conv_second, preferred_element_type=jnp.float32)
    grad_rows = (
        loss_scale
        * cot_rows.reshape(batch_size * frames, channels).astype(jnp.float32)
        * gelu_slope(pre_act)
    ).astype(jnp.bfloat16)
    grad_cols = jnp.dot(grad_rows, conv_second.T, preferred_element_type=jnp.float32).reshape(
        batch_size, frames, 3 * channels
    )
    first_taps = grad_cols[:, :, : 2 * channels].reshape(batch_size, 2 * frames, channels)
    late_tap = jnp.stack(
        [grad_cols[:, :, 2 * channels :], jnp.zeros((batch_size, frames, channels), jnp.float32)],
        axis=2,
    ).reshape(batch_size, 2 * frames, channels)
    grad_hidden = jnp.concatenate(
        [first_taps, jnp.zeros((batch_size, 1, channels), jnp.float32)], axis=1
    )
    grad_hidden = grad_hidden + jnp.concatenate(
        [jnp.zeros((batch_size, 2, channels), jnp.float32), late_tap[:, : 2 * frames - 1]], axis=1
    )
    grad_shift = grad_hidden * gelu_slope(shifted)
    gain_grad = jnp.sum(grad_shift * normed, axis=(0, 1))
    shift_grad = jnp.sum(grad_shift, axis=(0, 1))
    grad_scaled = grad_shift * norm_gain
    grad_pre = inv_std * (
        grad_scaled
        - jnp.mean(grad_scaled, axis=1, keepdims=True)
        - normed * jnp.mean(grad_scaled * normed, axis=1, keepdims=True)
    )
    grad_pre = grad_pre.astype(jnp.bfloat16).reshape(batch_size * first_len, channels)
    grad_first = jnp.dot(patches.T, grad_pre, preferred_element_type=jnp.float32)
    return (second_rows, grad_rows, grad_first, jnp.stack([gain_grad, shift_grad]))


def on_device(audio, counts, cotangent, conv_first, norm_gain, norm_bias, conv_second):
    groups = lax.axis_size("dx")
    position = lax.axis_index("dx")
    slot_count = audio.shape[1]
    receive = cotangent.shape[1]
    frames = cotangent.shape[2]
    all_counts = lax.all_gather(counts, "dx", axis=1, tiled=True)[0]
    starts = jnp.cumsum(all_counts, dtype=jnp.int32) - all_counts
    everything = lax.all_gather(audio, "dx", axis=1, tiled=True)[0]
    wanted = jnp.arange(receive, dtype=jnp.int32) * groups + position
    holder = (
        jnp.sum((starts[None, :] <= wanted[:, None]).astype(jnp.int32), axis=1, dtype=jnp.int32) - 1
    )
    offset = wanted - starts[holder]
    crop_waves = jnp.take(everything, holder * slot_count + offset, axis=0)
    loss_scale = 1.0 / math.sqrt(groups * lax.axis_size("dy") * receive * frames)
    second_rows, grad_rows, grad_first, grad_gains = forward_backward(
        crop_waves, cotangent[0], conv_first, norm_gain, norm_bias, conv_second, loss_scale
    )
    row_part = lax.psum_scatter(
        jnp.dot(second_rows.T, grad_rows, preferred_element_type=jnp.float32),
        "dy",
        scatter_dimension=0,
        tiled=True,
    )
    summed_first, summed_gains = lax.psum((grad_first, grad_gains), ("dx", "dy"))
    summed_second = lax.psum(row_part, "dx")
    return (summed_first, summed_gains, summed_second)


def solution(mesh):
    in_specs = (P("dy", "dx", None), P("dy", "dx"), P("dy", "dx", None, None), P(), P(), P(), P())
    out_specs = (P(), P(), P("dy", None))
    return jax.shard_map(
        on_device, mesh=mesh, in_specs=in_specs, out_specs=out_specs, check_vma=False
    )
```

profile of v0, /device:TPU:0, one launch (start us, length us, event | category | flops | bytes accessed | tf_op | source)
XLA Modules:
  0.0 161.6 jit_solution(16885701877535695636)
XLA Ops:
  9.9 8.9 %all-reduce.3 = s32[4]{0:T(128)S(1)} all-reduce(s32[4]{0:T(128)S(1)} %bitcast_dynamic-update-slice_fusion), channel_id=1, replica_groups=mesh['dx'=4,'dy'=8] {'dx'}, use_global_device_ids=true, to_apply=%add.3 | all-reduce | flops 4 | bytes 32 | tf_op jit(solution)/shard_map/squeeze | solution.py:80
  19.9 8.6 %all_gather.7 = bf16[1,32,2570]{2,1,0:T(8,128)(2,1)S(1)} all-gather(bf16[1,8,2570]{2,1,0:T(8,128)(2,1)} %param.7), channel_id=1, replica_groups=mesh['dx'=4,'dy'=8] {'dx'}, dimensions={1}, use_global_device_ids=true | all-gather | bytes 205600 | tf_op jit(solution)/shard_map/all_gather | solution.py:82
  30.6 1.5 fusion.27
  32.8 1.3 copy-done.1
  34.1 2.4 %multiply_convert_fusion.1 = bf16[4,513,512]{2,1,0:T(8,128)(2,1)} fusion(f32[512]{0:T(512)S(1)} %copy-done.6, f32[512]{0:T(512)S(1)} %copy-done.5, f32[4,512]{1,0:T(4,128)S(1)} %add_rsqrt_fusion, f32[4,513,512]{2,1,0:T(8,128)S(1)} %get-tuple-element.13, f32[4,512]{1,0:T(4,128)S(1)} %broadcast_multiply_fusion.2), kind=kLoop, calls=%fused_computation.11 | loop fusion | flops 9455616 | bytes 6324224 | tf_op jit(solution)/shard_map/convert_element_type | solution.py:34
  36.5 11.7 %slice.24 = bf16[4,256,512]{2,1,0:T(8,128)(2,1)} slice(bf16[4,513,512]{2,1,0:T(8,128)(2,1)} %multiply_convert_fusion.1), slice={[0:4:1], [2:513:2], [0:512:1]} | slice | bytes 2097152 | tf_op jit(solution)/shard_map/slice | solution.py:36
  48.2 3.1 %slice.34 = bf16[4,512,512]{2,1,0:T(8,128)(2,1)} slice(bf16[4,513,512]{2,1,0:T(8,128)(2,1)} %multiply_convert_fusion.1), slice={[0:4], [0:512], [0:512]} | slice | bytes 4194304 | tf_op jit(solution)/shard_map/slice | solution.py:35
  51.3 1.6 %convert_multiply_fusion = f32[1,4,256,512]{3,2,1,0:T(8,128)} fusion(bf16[1,4,256,512]{3,2,1,0:T(8,128)(2,1)S(1)} %copy-done.3), kind=kLoop, calls=%fused_computation.26 | loop fusion | flops 1048576 | bytes 3145728 | tf_op jit(solution)/shard_map/mul | solution.py:42
  52.9 4.1 %concatenate.20 = bf16[1024,1024]{1,0:T(8,128)(2,1)} reshape(bf16[4,512,512]{2,1,0:T(8,128)(2,1)} %slice.34) | data formatting | bytes 4194304 | tf_op jit(solution)/shard_map/concatenate | solution.py:37
  57.0 5.1 %fusion.11 = bf16[1024,512]{1,0:T(8,128)(2,1)S(1)} fusion(f32[1,4,256,512]{3,2,1,0:T(8,128)} %convert_multiply_fusion, bf16[1536,512]{1,0:T(8,128)(2,1)S(1)} %copy-done, bf16[1024,512]{1,0:T(8,128)(2,1)} %bitcast.53, bf16[1024,1024]{1,0:T(8,128)(2,1)} %concatenate.20), kind=kOutput, calls=%fused_computation.25 | convolution fusion | flops 1622147072 | bytes 7864320 | tf_op jit(solution)/shard_map/dot_general | solution.py:40
  62.0 3.5 %fusion.12 = f32[1536,512]{1,0:T(8,128)} fusion(bf16[1024,512]{1,0:T(8,128)(2,1)S(1)} %fusion.11, bf16[1024,512]{1,0:T(8,128)(2,1)S(1)} %bitcast.54, bf16[1024,1024]{1,0:T(8,128)(2,1)S(1)} %copy-done.2), kind=kOutput, calls=%fused_computation.27 | convolution fusion | flops 1616904192 | bytes 7340032 | tf_op jit(solution)/shard_map/dot_general | solution.py:94
  65.8 1.8 %fusion.28 = f32[1024,1536]{1,0:T(8,128)S(1)} fusion(bf16[1024,512]{1,0:T(8,128)(2,1)S(1)} %fusion.11, bf16[1536,512]{1,0:T(8,128)(2,1)S(1)} %copy-done), kind=kOutput, calls=%fused_computation.63 | convolution fusion | flops 1610612736 | bytes 8912896 | tf_op jit(solution)/shard_map/dot_general | solution.py:46
  67.7 1.5 slice.36
  69.2 2.4 %slice.35 = f32[4,256,1024]{2,1,0:T(8,128)} slice(f32[4,256,1536]{2,1,0:T(8,128)S(1)} %bitcast.52), slice={[0:4], [0:256], [0:1024]} | slice | bytes 8388608 | tf_op jit(solution)/shard_map/slice | solution.py:49
  71.6 5.0 %reshape.144 = f32[4,512,512]{2,1,0:T(8,128)} reshape(f32[4,256,1024]{2,1,0:T(8,128)} %slice.35) | data formatting | bytes 8388608 | tf_op jit(solution)/shard_map/reshape | solution.py:49
  76.6 3.0 %stack.15 = f32[4,256,1,512]{3,2,1,0:T(1,128)S(1)} reshape(f32[4,256,512]{2,1,0:T(8,128)} %slice.36) | data formatting | bytes 4194304 | tf_op jit(solution)/shard_map/stack | solution.py:50
  79.6 3.4 %stack.16 = f32[4,256,2,512]{3,2,1,0:T(2,128)} pad(f32[4,256,1,512]{3,2,1,0:T(1,128)S(1)} %stack.15, f32[]{:T(128)} %constant.27.clone.1), padding=0_0x0_0x0_1x0_0 | pad | bytes 6291460 | tf_op jit(solution)/shard_map/stack | solution.py:50
  83.0 6.1 %reshape.145 = f32[4,512,512]{2,1,0:T(8,128)} reshape(f32[4,256,2,512]{3,2,1,0:T(2,128)} %stack.16) | data formatting | bytes 8388608 | tf_op jit(solution)/shard_map/reshape | solution.py:53
  89.1 9.3 %multiply_reduce_fusion = (f32[512]{0:T(512)S(1)}, f32[4,512]{1,0:T(4,128)S(1)}, f32[4,512]{1,0:T(4,128)S(1)}, f32[512]{0:T(512)S(1)}, f32[4,513,512]{2,1,0:T(8,128)}) fusion(f32[4,512]{1,0:T(4,128)S(1)} %add_rsqrt_fusion, f32[4,513,512]{2,1,0:T(8,128)} %copy-done.1, f32[4,512]{1,0:T(4,128)S(1)} %broadcast_multiply_fusion.2, f32[512]{0:T(512)S(1)} %copy-done.5, ...), kind=kLoop, calls=%fused_computation.8 | loop fusion | flops 22057984 | bytes 16826368 | tf_op jit(solution)/shard_map/reduce_sum | solution.py:61
  98.5 7.9 %reduce-scatter.2.cloned.1.call-done = f32[192,512]{1,0:T(8,128)} async-done(((f32[1536,512]{1,0:T(8,128)}), f32[192,512]{1,0:T(8,128)}) %reduce-scatter.2.cloned.1.call-update) | async-done | bytes 393232 | tf_op jit(solution)/shard_map/reduce_scatter | solution.py:93
  106.4 4.7 %fusion.14 = f32[10,512]{1,0:T(8,128)S(1)} fusion(f32[4,513,512]{2,1,0:T(8,128)} %get-tuple-element.9, f32[4,512]{1,0:T(4,128)S(1)} %get-tuple-element.14, f32[4,512]{1,0:T(4,128)S(1)} %get-tuple-element.15, f32[512]{0:T(512)S(1)} %copy-done.5, f32[4,512]{1,0:T(4,128)S(1)} %add_rsqrt_fusion, f32[4,513,512]{2,1,0:T(8,128)} %copy-done.1, ...), kind=kOutput, calls=%fused_computation.29 | convolution fusion | flops 29499552 | bytes 8501328 | tf_op jit(solution)/shard_map/dot_general | solution.py:70
  111.1 38.7 %all-reduce.4 = (f32[10,512]{1,0:T(8,128)}, f32[2,512]{1,0:T(2,128)}) all-reduce(f32[10,512]{1,0:T(8,128)S(1)} %fusion.14, f32[2,512]{1,0:T(2,128)S(1)} %pad_maximum_fusion.8), channel_id=1, replica_groups=mesh['dx'=4,'dy'=8] {'dx','dy'}, use_global_device_ids=true, to_apply=%region_6.7 | all-reduce | flops 6144 | bytes 49152 | tf_op jit(solution)/shard_map/psum | solution.py:99
  149.9 3.2 %all-reduce.7.cloned.1.call-done = f32[192,512]{1,0:T(8,128)} async-done(((f32[192,512]{1,0:T(8,128)}), f32[192,512]{1,0:T(8,128)}) %all-reduce.7.cloned.1.call-update) | async-done | bytes 393232 | tf_op jit(solution)/shard_map/psum | solution.py:100
  153.0 1.8 %copy.17 = f32[192,512]{1,0:T(8,128)} copy(f32[192,512]{1,0:T(8,128)} %all-reduce.7.cloned.1.call-done) | data formatting | bytes 786432
  (43 shorter events, 6.0 us)
Async XLA Ops:
  7.2 49.8 %copy-start = (bf16[1536,512]{1,0:T(8,128)(2,1)S(1)}, bf16[1536,512]{1,0:T(8,128)(2,1)}, u32[]{:S(2)}) copy-start(bf16[1536,512]{1,0:T(8,128)(2,1)} %param.13) | copy-start | bytes 4718596
  7.2 99.2 %reduce-scatter.2.cloned.1.call-start = ((), (), s32[]{:S(2)}) async-start(), calls=%async_computation.1 | async-start | bytes 3538944 | tf_op jit(solution)/shard_map/reduce_scatter | solution.py:93
  30.6 3.5 %copy-start.5 = (f32[512]{0:T(512)S(1)}, f32[512]{0:T(512)}, u32[]{:S(2)}) copy-start(f32[512]{0:T(512)} %param.11) | copy-start | bytes 6148
  30.6 3.5 %copy-start.6 = (f32[512]{0:T(512)S(1)}, f32[512]{0:T(512)}, u32[]{:S(2)}) copy-start(f32[512]{0:T(512)} %param.12) | copy-start | bytes 6148
  32.2 2.0 %copy-start.1 = (f32[4,513,512]{2,1,0:T(8,128)}, f32[4,513,512]{2,1,0:T(8,128)S(1)}, u32[]{:S(2)}) copy-start(f32[4,513,512]{2,1,0:T(8,128)S(1)} %get-tuple-element.13) | copy-start | bytes 12607492
  36.5 14.7 %copy-start.3 = (bf16[1,4,256,512]{3,2,1,0:T(8,128)(2,1)S(1)}, bf16[1,4,256,512]{3,2,1,0:T(8,128)(2,1)}, u32[]{:S(2)}) copy-start(bf16[1,4,256,512]{3,2,1,0:T(8,128)(2,1)} %param.9) | copy-start | bytes 3145732
  57.0 5.1 %copy-start.2 = (bf16[1024,1024]{1,0:T(8,128)(2,1)S(1)}, bf16[1024,1024]{1,0:T(8,128)(2,1)}, u32[]{:S(2)}) copy-start(bf16[1024,1024]{1,0:T(8,128)(2,1)} %concatenate.20) | copy-start | bytes 6291460
  57.0 5.1 %copy-start.4 = (bf16[4,256,512]{2,1,0:T(8,128)(2,1)S(1)}, bf16[4,256,512]{2,1,0:T(8,128)(2,1)}, u32[]{:S(2)}) copy-start(bf16[4,256,512]{2,1,0:T(8,128)(2,1)} %slice.24) | copy-start | bytes 3145732
  65.6 87.4 %all-reduce.7.cloned.1.call-start = ((), (), s32[]{:S(2)}) async-start(), calls=%async_computation.2 | async-start | bytes 786432 | tf_op jit(solution)/shard_map/psum | solution.py:100
Sparse Core Ops, SparseCore 0:
  65.7 40.6 reduce-scatter.1
  109.3 43.6 all-reduce.6
where the time goes:
time: 163 us; the launch traced here: 162 us
  blocking collectives  56.3 us (35%)
  local copies, waits for them, and re-layouts  48 us (29%)
  matrix products  16.6 us (10%)
  between operations  14.9 us (9%)
  other arithmetic  14.4 us (9%)
  waiting for transfers between devices  11.1 us (7%)
    psum x1, blocking collectives, on_device(): lax.psum((grad_first, grad_gains), ('dx', 'dy'))  38.7 us
    slice x1, local copies, waits for them, and re-layouts, forward_backward(): third_tap = hidden[:, 2::2]  11.7 us
    reduce_sum x1, other arithmetic, forward_backward(): gain_grad = jnp.sum(grad_shift * normed, axis=(0, 1))  9.31 us
    squeeze x1, blocking collectives, on_device(): all_counts = lax.all_gather(counts, 'dx', axis=1, tiled=True)[0]  8.88 us
    all_gather x1, blocking collectives, on_device(): everything = lax.all_gather(audio, 'dx', axis=1, tiled=True)[0]  8.63 us
    reduce_scatter x1, waiting for transfers between devices, on_device(): lax.psum_scatter(jnp.dot(second_rows.T, grad_rows, preferred_element_type...  7.93 us
    another operation x2, local copies, waits for them, and re-layouts, forward_backward(): jnp.stack([grad_cols[:, :, 2 * channels:], jnp.zeros((batch_size, frames,...  6.46 us
    reshape x1, local copies, waits for them, and re-layouts, forward_backward(): late_tap = jnp.stack([grad_cols[:, :, 2 * channels:], jnp.zeros((batch_si...  6.07 us
  transfers between devices with their start and end apart: 2, of which 2 were waited for; matrix products, arithmetic and copies ran while one was open for 23% of the time, Pallas kernels for 0%

commit v1 on v0

v1 whole, which is shorter than its diff:
```python
import functools
import math

import jax
import jax.numpy as jnp
from jax import lax
from jax.experimental import pallas as pl
from jax.experimental.pallas import tpu as pltpu
from jax.sharding import PartitionSpec as P

BF16 = jnp.bfloat16
F32 = jnp.float32
LANES = 128
ROWS = 32
VMEM_SPEC = pl.BlockSpec(memory_space=pltpu.VMEM)
SMEM_SPEC = pl.BlockSpec(memory_space=pltpu.SMEM)


def gelu_cdf(value):
    return 0.5 * (1.0 + lax.erf(value * 0.7071067811865476))


def gelu_slope(value):
    return gelu_cdf(value) + value * jnp.exp(-0.5 * value * value) * 0.3989422804014327


def chunk(index, rows=ROWS):
    return pl.ds(pl.multiple_of(index * rows, rows), rows)


def fold(rows):
    total = rows[0:8]
    for start in range(8, rows.shape[0], 8):
        total = total + rows[start : start + 8]
    return total


def forward_kernel(
    peers, slots, crops, frames, channels, block, loss_scale, where, *refs
):
    buffers = refs[:peers]
    (cot, taps, second, gain, bias, keep, send, grad_rows, patches, stats) = refs[
        peers : peers + 10
    ]
    (waves, wave_rows, even, odd, hid, rows, pre, acc) = refs[peers + 10 :]
    crop = pl.program_id(0)
    samples = 10 * (frames + 1)
    first_len = 2 * frames + 1
    own = where[0]
    core = where[1]
    wanted = waves.shape[0]

    @pl.when(crop == 0)
    def _():
        counts = [buffer[0:1, samples : samples + 1].astype(F32) for buffer in buffers]
        slot = lax.broadcasted_iota(jnp.int32, (wanted, slots), 1)
        number = lax.broadcasted_iota(jnp.int32, (wanted, slots), 0) * peers + own
        picked = jnp.zeros(waves.shape, F32)
        for k in range(peers):
            holder = jnp.bitwise_xor(own, k)
            start = jnp.zeros((1, 1), F32)
            for other in range(peers):
                before = jnp.bitwise_xor(own, other) < holder
                start = start + jnp.where(before, counts[other], 0.0)
            first = jnp.broadcast_to(start.astype(jnp.int32), (wanted, slots))
            live = jnp.broadcast_to(counts[k].astype(jnp.int32), (wanted, slots))
            hit = (first + slot == number) & (slot < live)
            one_hot = jnp.where(hit, 1.0, 0.0).astype(BF16)
            picked = picked + jnp.dot(
                one_hot, buffers[k][...], preferred_element_type=F32
            )
        waves[...] = picked
        acc[...] = jnp.zeros_like(acc)

    period = 5 * LANES
    per_block = period // 10
    at = lax.broadcasted_iota(jnp.int32, (period, LANES), 0) % 10
    spread = jnp.where(
        at == lax.broadcasted_iota(jnp.int32, (period, LANES), 1), 1.0, 0.0
    ).astype(BF16)
    lane = lax.broadcasted_iota(jnp.int32, (per_block, period), 1)
    low = lax.broadcasted_iota(jnp.int32, (per_block, period), 0) * 10
    mask = (lane >= low) & (lane < low + 10)
    wave = waves[pl.ds(crop, 1), :]
    for part in range(10 * frames // period):
        piece = jnp.broadcast_to(
            wave[:, part * period : (part + 1) * period], (per_block, period)
        )
        piece = jnp.where(mask, piece, 0.0).astype(BF16)
        wave_rows[part * per_block : (part + 1) * per_block] = jnp.dot(
            piece, spread, preferred_element_type=F32
        )
    last = jnp.broadcast_to(wave[:, 10 * frames : 10 * frames + LANES], (16, LANES))
    last_row = lax.broadcasted_iota(jnp.int32, (16, LANES), 0)
    last_lane = lax.broadcasted_iota(jnp.int32, (16, LANES), 1)
    wave_rows[frames : frames + 16] = jnp.where((last_row == 0) & (last_lane < 10), last, 0.0)
    long = frames + 8
    both = wave_rows[0:long] + pltpu.roll(wave_rows[1 : long + 1], 10, 1)
    patch = both.astype(BF16)
    patches[0] = patch

    first = jnp.dot(patch, taps[:, :channels], preferred_element_type=F32)
    even[...] = first
    total = fold(first)
    first = jnp.dot(patch[:frames], taps[:, channels:], preferred_element_type=F32)
    odd[...] = first
    total = total + fold(first)
    mean = jnp.sum(total, axis=0, keepdims=True) * (1.0 / first_len)
    tail_row = lax.broadcasted_iota(jnp.int32, (8, channels), 0) == 0

    def squares(i, total):
        a = even[chunk(i)] - mean
        b = odd[chunk(i)] - mean
        return total + fold(a * a + b * b)

    tail = even[frames:long] - mean
    total = lax.fori_loop(
        0, frames // ROWS, squares, jnp.where(tail_row, tail * tail, 0.0), unroll=True
    )
    var = jnp.sum(total, axis=0, keepdims=True) * (1.0 / first_len)
    inv_std = lax.rsqrt(var + 1e-05)
    stats[0, 0:1] = mean
    stats[0, 1:2] = inv_std
    scale = gain[...]
    shift = bias[...]

    def hidden(centre):
        value = centre * inv_std * scale + shift
        return value * gelu_cdf(value)

    def hide(i, carry):
        value = hidden(even[chunk(i)] - mean)
        hid[chunk(i)] = value
        rows[chunk(i), 0:channels] = value.astype(BF16)
        rows[chunk(i), channels : 2 * channels] = hidden(odd[chunk(i)] - mean).astype(BF16)
        return carry

    lax.fori_loop(0, frames // ROWS, hide, 0, unroll=True)
    hid[frames:long] = hidden(tail)
    rows[:, 2 * channels :] = hid[1 : frames + 1].astype(BF16)

    pre[...] = jnp.dot(rows[...], second[...], preferred_element_type=F32)

    def slope(i, carry):
        value = loss_scale * cot[0, chunk(i)].astype(F32) * gelu_slope(pre[chunk(i)])
        grad_rows[0, chunk(i)] = value.astype(BF16)
        return carry

    lax.fori_loop(0, frames // ROWS, slope, 0, unroll=True)
    acc[...] += lax.dot_general(
        rows[...],
        grad_rows[0],
        (((0,), (0,)), ((), ())),
        preferred_element_type=F32,
    )

    @pl.when(crop == crops - 1)
    def _():
        for pair in range(acc.shape[0] // (2 * block)):
            mine = pl.ds(pl.multiple_of((2 * pair + core) * block, block), block)
            theirs = pl.ds(pl.multiple_of((2 * pair + 1 - core) * block, block), block)
            keep[pair * block : (pair + 1) * block] = acc[mine]
            send[pair * block : (pair + 1) * block] = acc[theirs].astype(BF16)


def forward(where, buffers, cot, taps, second, gain, bias, block, loss_scale):
    peers = len(buffers)
    slots, width = buffers[0].shape
    crops, frames, channels = cot.shape
    long = frames + 8
    half = second.shape[0] // 2

    def whole(array):
        return pl.BlockSpec(array.shape, lambda i: (0,) * array.ndim)

    def per_crop(*shape):
        return pl.BlockSpec((1, *shape), lambda i: (i, 0, 0))

    return pl.pallas_call(
        functools.partial(
            forward_kernel, peers, slots, crops, frames, channels, block, loss_scale
        ),
        grid=(crops,),
        in_specs=[
            SMEM_SPEC,
            *[whole(b) for b in buffers],
            per_crop(frames, channels),
            whole(taps),
            whole(second),
            whole(gain),
            whole(bias),
        ],
        out_specs=[
            pl.BlockSpec((half, channels), lambda i: (0, 0)),
            pl.BlockSpec((half, channels), lambda i: (0, 0)),
            per_crop(frames, channels),
            per_crop(long, LANES),
            per_crop(8, channels),
        ],
        out_shape=[
            jax.ShapeDtypeStruct((half, channels), F32),
            jax.ShapeDtypeStruct((half, channels), BF16),
            jax.ShapeDtypeStruct((crops, frames, channels), BF16),
            jax.ShapeDtypeStruct((crops, long, LANES), BF16),
            jax.ShapeDtypeStruct((crops, 8, channels), F32),
        ],
        scratch_shapes=[
            pltpu.VMEM((max(8, crops), width), F32),
            pltpu.VMEM((frames + 16, LANES), F32),
            pltpu.VMEM((long, channels), F32),
            pltpu.VMEM((frames, channels), F32),
            pltpu.VMEM((long, channels), F32),
            pltpu.VMEM((frames, 3 * channels), BF16),
            pltpu.VMEM((frames, channels), F32),
            pltpu.VMEM(second.shape, F32),
        ],
        name="forward",
        compiler_params=pltpu.CompilerParams(vmem_limit_bytes=32 << 20),
    )(where, *buffers, cot, taps, second, gain, bias)


def backward_kernel(
    crops, frames, channels, grad_rows, patches, stats, taps, second, gain, bias,
    small, even, odd, cols, grad_even, grad_odd, late, first_acc, gains_acc,
):
    crop = pl.program_id(0)
    long = frames + 8
    first_len = 2 * frames + 1

    @pl.when(crop == 0)
    def _():
        first_acc[...] = jnp.zeros_like(first_acc)
        gains_acc[...] = jnp.zeros_like(gains_acc)

    patch = patches[0]
    even[...] = jnp.dot(patch, taps[:, :channels], preferred_element_type=F32)
    odd[...] = jnp.dot(patch[:frames], taps[:, channels:], preferred_element_type=F32)
    cols[...] = lax.dot_general(
        grad_rows[0],
        second[: 2 * channels],
        (((1,), (1,)), ((), ())),
        preferred_element_type=F32,
    )
    late[0:8] = jnp.zeros((8, channels), F32)
    late[8 : frames + 8] = lax.dot_general(
        grad_rows[0],
        second[2 * channels :],
        (((1,), (1,)), ((), ())),
        preferred_element_type=F32,
    )
    mean = stats[0, 0:1]
    inv_std = stats[0, 1:2]
    scale = gain[...]
    shift = bias[...]

    def shift_grad(pre_norm, grad_hidden):
        normed = (pre_norm - mean) * inv_std
        grad = grad_hidden * gelu_slope(normed * scale + shift)
        return normed, grad

    def first_pass(i, carry):
        shifts, gains = carry
        normed, grad = shift_grad(
            even[chunk(i)], cols[chunk(i), 0:channels] + late[pl.ds(i * ROWS + 7, ROWS), :]
        )
        even[chunk(i)] = normed
        grad_even[chunk(i)] = grad
        shifts = shifts + fold(grad)
        gains = gains + fold(grad * normed)
        normed, grad = shift_grad(odd[chunk(i)], cols[chunk(i), channels:])
        odd[chunk(i)] = normed
        grad_odd[chunk(i)] = grad
        return shifts + fold(grad), gains + fold(grad * normed)

    tail_row = lax.broadcasted_iota(jnp.int32, (8, channels), 0) == 0
    tail_normed, tail_grad = shift_grad(
        even[frames:long],
        jnp.broadcast_to(late[frames + 7 : frames + 8], (8, channels)),
    )
    tail_grad = jnp.where(tail_row, tail_grad, 0.0)
    carry = (tail_grad, tail_grad * tail_normed)
    for i in range(frames // ROWS):
        carry = first_pass(i, carry)
    shifts = jnp.sum(carry[0], axis=0, keepdims=True)
    gains = jnp.sum(carry[1], axis=0, keepdims=True)
    gains_acc[0:1] += gains
    gains_acc[1:2] += shifts
    shifts = shifts * (1.0 / first_len)
    gains = gains * (1.0 / first_len)
    outer = inv_std * scale

    def grad_pre(grad, normed):
        return (outer * (grad - shifts - normed * gains)).astype(BF16)

    tail_pre = jnp.where(tail_row, outer * (tail_grad - shifts - tail_normed * gains), 0.0)
    grads = [grad_pre(grad_even[chunk(i)], even[chunk(i)]) for i in range(frames // ROWS)]
    whole_even = jnp.concatenate(grads, axis=0)
    grads = [grad_pre(grad_odd[chunk(i)], odd[chunk(i)]) for i in range(frames // ROWS)]
    whole_odd = jnp.concatenate(grads, axis=0)

    def outer_sum(a, b):
        return lax.dot_general(a, b, (((0,), (0,)), ((), ())), preferred_element_type=F32)

    first_acc[0:LANES] += outer_sum(patch[:frames], whole_even) + outer_sum(
        patch[frames:long], tail_pre.astype(BF16)
    )
    first_acc[LANES:] += outer_sum(patch[:frames], whole_odd)

    @pl.when(crop == crops - 1)
    def _():
        small[...] = jnp.zeros_like(small)
        small[0:10] = first_acc[0:10] + first_acc[LANES + 5 : LANES + 15]
        small[10:12] = gains_acc[0:2]


def backward(grad_rows, patches, stats, taps, second, gain, bias):
    crops, frames, channels = grad_rows.shape
    long = frames + 8

    def whole(array):
        return pl.BlockSpec(array.shape, lambda i: (0,) * array.ndim)

    def per_crop(array):
        return pl.BlockSpec((1, *array.shape[1:]), lambda i: (i, 0, 0))

    return pl.pallas_call(
        functools.partial(backward_kernel, crops, frames, channels),
        grid=(crops,),
        in_specs=[
            per_crop(grad_rows),
            per_crop(patches),
            per_crop(stats),
            whole(taps),
            whole(second),
            whole(gain),
            whole(bias),
        ],
        out_specs=pl.BlockSpec((16, channels), lambda i: (0, 0)),
        out_shape=jax.ShapeDtypeStruct((16, channels), F32),
        scratch_shapes=[
            pltpu.VMEM((long, channels), F32),
            pltpu.VMEM((frames, channels), F32),
            pltpu.VMEM((frames, 2 * channels), F32),
            pltpu.VMEM((frames, channels), F32),
            pltpu.VMEM((frames, channels), F32),
            pltpu.VMEM((long, channels), F32),
            pltpu.VMEM((2 * LANES, channels), F32),
            pltpu.VMEM((8, channels), F32),
        ],
        name="backward",
        compiler_params=pltpu.CompilerParams(vmem_limit_bytes=32 << 20),
    )(grad_rows, patches, stats, taps, second, gain, bias)


def tree(values):
    while len(values) > 1:
        values = [values[i] + values[i + 1] for i in range(0, len(values), 2)]
    return values[0]


def swap(value, axis, key):
    return lax.ppermute(value, axis, [(i, i ^ key) for i in range(lax.axis_size(axis))])


def parts(value):
    high = value.astype(BF16)
    low = (value - high.astype(F32)).astype(BF16)
    return high, low


def kernel_call(kernel, where, arrays, out_shape, name):
    return pl.pallas_call(
        kernel,
        in_specs=[SMEM_SPEC] + [VMEM_SPEC] * len(arrays),
        out_specs=jax.tree.map(lambda _: VMEM_SPEC, out_shape),
        out_shape=out_shape,
        name=name,
    )(where, *arrays)


def split_dx(where, keep, received, peers, block):
    half, channels = keep.shape
    groups = half // block
    rows = block // peers
    if rows % 16:
        total = (keep + received.astype(F32)).reshape(groups, peers, rows, channels)
        picked = [
            lax.dynamic_index_in_dim(total, where[0] ^ k, axis=1, keepdims=False)
            for k in range(peers)
        ]
        picked = [p.reshape(groups * rows, channels) for p in picked]
        return [picked[0]] + [p.astype(BF16) for p in picked[1:]]

    def body(where, keep, received, *outs):
        for k in range(peers):
            part = jnp.bitwise_xor(where[0], k)
            for g in range(groups):
                at = pl.ds(pl.multiple_of(g * block + part * rows, rows), rows)
                value = keep[at] + received[at].astype(F32)
                outs[k][g * rows : (g + 1) * rows] = value.astype(outs[k].dtype)

    shape = (groups * rows, channels)
    return kernel_call(
        body,
        where,
        (keep, received),
        [jax.ShapeDtypeStruct(shape, BF16 if k else F32) for k in range(peers)],
        "split_dx",
    )


def split_dy(where, own, received, small, small_received, groups):
    rows = own.shape[0] // groups
    channels = own.shape[1]
    extra = small.shape[0]
    if rows % 16:
        total = tree([own] + [r.astype(F32) for r in received])
        total = total.reshape(groups, rows, channels)
        high, low = parts(small + small_received)
        picked = [
            lax.dynamic_index_in_dim(total, where[2] ^ k, axis=0, keepdims=False)
            for k in range(groups)
        ]
        first = jnp.concatenate([picked[0], high.astype(F32), low.astype(F32)], axis=0)
        return [first] + [
            jnp.concatenate([p.astype(BF16), high, low], axis=0) for p in picked[1:]
        ]

    def body(where, own, small, small_received, *refs):
        received, outs = refs[: len(refs) - groups], refs[len(refs) - groups :]
        high, low = parts(small[...] + small_received[...])
        for k in range(groups):
            at = pl.ds(pl.multiple_of(jnp.bitwise_xor(where[2], k) * rows, rows), rows)
            value = tree([own[at]] + [r[at].astype(F32) for r in received])
            kind = outs[k].dtype
            outs[k][0:rows] = value.astype(kind)
            outs[k][rows : rows + extra] = high.astype(kind)
            outs[k][rows + extra :] = low.astype(kind)

    shape = (rows + 2 * extra, channels)
    return kernel_call(
        body,
        where,
        (own, small, small_received, *received),
        [jax.ShapeDtypeStruct(shape, BF16 if k else F32) for k in range(groups)],
        "split_dy",
    )


def add_dy(where, own, received, extra):
    rows = own.shape[0] - 2 * extra

    def add(own, received):
        big = tree([own[:rows]] + [r[:rows].astype(F32) for r in received])
        small = tree(
            [v[rows : rows + extra].astype(F32) + v[rows + extra :].astype(F32)
             for v in (own, *received)]
        )
        high, low = parts(small)
        return big.astype(BF16), high, low

    if rows % 16:
        return jnp.concatenate(add(own, received), axis=0)

    def body(where, own, *refs):
        big, high, low = add(own[...], [r[...] for r in refs[:-1]])
        refs[-1][0:rows] = big
        refs[-1][rows : rows + extra] = high
        refs[-1][rows + extra :] = low

    return kernel_call(
        body,
        where,
        (own, *received),
        jax.ShapeDtypeStruct(own.shape, BF16),
        "add_dy",
    )


def assemble(where, pieces, extra):
    peers = len(pieces)
    rows = pieces[0].shape[0] - 2 * extra
    channels = pieces[0].shape[1]

    def small_sum(values):
        return tree(
            [v[rows : rows + extra].astype(F32) + v[rows + extra :].astype(F32) for v in values]
        )

    if rows % 16:
        stacked = jnp.stack([p[:rows] for p in pieces])
        order = jnp.arange(peers, dtype=jnp.int32) ^ where[0]
        second = jnp.take(stacked, order, axis=0).reshape(peers * rows, channels)
        small = small_sum(pieces)
        return small[:10], small[10:12], second.astype(F32)

    def body(where, *refs):
        values, (first, gains, second) = refs[:peers], refs[peers:]
        small = small_sum([v[...] for v in values])
        first[...] = small[0:10]
        gains[...] = small[10:12]
        for k in range(peers):
            at = pl.ds(pl.multiple_of(jnp.bitwise_xor(where[0], k) * rows, rows), rows)
            second[at] = values[k][0:rows].astype(F32)

    return kernel_call(
        body,
        where,
        pieces,
        [
            jax.ShapeDtypeStruct((10, channels), F32),
            jax.ShapeDtypeStruct((2, channels), F32),
            jax.ShapeDtypeStruct((peers * rows, channels), F32),
        ],
        "assemble",
    )


def on_device(audio, counts, cotangent, conv_first, norm_gain, norm_bias, conv_second):
    peers = lax.axis_size("dx")
    members = lax.axis_size("dy")
    groups = members // 2
    own = lax.axis_index("dx")
    line = lax.axis_index("dy")
    where = jnp.stack([own, line % 2, line // 2]).astype(jnp.int32)
    crops, frames, channels = cotangent.shape[1:]
    slots = audio.shape[1]
    block = conv_second.shape[0] // members
    loss_scale = 1.0 / math.sqrt(peers * members * crops * frames)

    held = jnp.broadcast_to(counts.astype(BF16), (slots, 1))
    samples = audio.shape[2]
    packed = jnp.concatenate([audio[0], held], axis=1)
    packed = jnp.pad(packed, ((0, 0), (0, -(samples + 1) % LANES)))
    buffers = [packed] + [swap(packed, "dx", k) for k in range(1, peers)]

    taps = jnp.zeros((LANES, 2 * channels), BF16)
    taps = taps.at[0:10, :channels].set(conv_first).at[5:15, channels:].set(conv_first)
    gain = norm_gain.reshape(1, channels)
    bias = norm_bias.reshape(1, channels)

    keep, send, grad_rows, patches, stats = forward(
        where, buffers, cotangent[0], taps, conv_second, gain, bias, block, loss_scale
    )
    received = swap(send, "dy", 1)
    pieces = split_dx(where, keep, received, peers, block)
    received = [swap(pieces[k], "dx", k) for k in range(1, peers)]
    small = backward(grad_rows, patches, stats, taps, conv_second, gain, bias)
    small_received = swap(small, "dy", 1)
    pieces = split_dy(where, pieces[0], received, small, small_received, groups)
    received = [swap(pieces[k], "dy", 2 * k) for k in range(1, groups)]
    final = add_dy(where, pieces[0], received, small.shape[0])
    pieces = [final] + [swap(final, "dx", k) for k in range(1, peers)]
    return tuple(assemble(where, pieces, small.shape[0]))


def solution(mesh):
    in_specs = (P("dy", "dx", None), P("dy", "dx"), P("dy", "dx", None, None), P(), P(), P(), P())
    out_specs = (P(), P(), P("dy", None))
    return jax.shard_map(
        on_device, mesh=mesh, in_specs=in_specs, out_specs=out_specs, check_vma=False
    )
```

time: 163 us -> 69.8 us (0.43)
  blocking collectives: 56.3 us -> 0 us
  local copies, waits for them, and re-layouts: 48 us -> 10 us
  Pallas kernels: 0 us -> 24.6 us
  matrix products: 16.6 us -> 0 us
  starting transfers between devices: 0.26 us -> 16 us
  other arithmetic: 14.4 us -> 0.87 us
  between operations: 14.9 us -> 1.39 us
  waiting for transfers between devices: 11.1 us -> 16.4 us
    psum x1 -> x0, blocking collectives: 38.7 us -> none  [on_device(): lax.psum((grad_first, grad_gains), ('dx', 'dy'))]
    pallas_call x0 -> x6, Pallas kernels: none -> 24.6 us  [the longest x1 10.6 us: forward(): pl.pallas_call(functools.partial(forward_kernel, peers, slots, crops, fra...]
    slice x5 -> x0, local copies, waits for them, and re-layouts: 18.7 us -> none  [the longest x1 11.7 us: forward_backward(): third_tap = hidden[:, 2::2]]
    dot_general x5 -> x0, matrix products: 16.6 us -> none  [the longest x1 5.06 us: forward_backward(): jnp.dot(second_rows, conv_second, preferred_element_type=jnp.float32)]
    ppermute x0 -> x14, waiting for transfers between devices: none -> 16.4 us  [swap(): lax.ppermute(value, axis, [(i, i ^ key) for i in range(lax.axis_size(axis...]
    ppermute x0 -> x14, starting transfers between devices: none -> 16 us  [swap(): lax.ppermute(value, axis, [(i, i ^ key) for i in range(lax.axis_size(axis...]
    reshape x6 -> x0, local copies, waits for them, and re-layouts: 12.4 us -> none  [the longest x1 6.07 us: forward_backward(): late_tap = jnp.stack([grad_cols[:, :, 2 * channels:], jnp.zeros((batch_si...]
    reduce_sum x3 -> x0, other arithmetic: 10.1 us -> none  [the longest x1 9.31 us: forward_backward(): gain_grad = jnp.sum(grad_shift * normed, axis=(0, 1))]
  transfers between devices with their start and end apart: 2 -> 14, of which waited for: 2 -> 12; matrix products, arithmetic and copies ran while one was open for 23% -> 4% of each run, Pallas kernels for 0% -> 8%
where the time goes in v1:
time: 69.8 us; the launch traced here: 69.2 us
  Pallas kernels  24.6 us (35%)
  waiting for transfers between devices  16.4 us (23%)
  starting transfers between devices  16 us (23%)
  local copies, waits for them, and re-layouts  10 us (14%)
  between operations  1.39 us (2%)
  other arithmetic  0.87 us (1%)
    ppermute x14, waiting for transfers between devices, swap(): lax.ppermute(value, axis, [(i, i ^ key) for i in range(lax.axis_size(axis...  16.4 us
    ppermute x14, starting transfers between devices, swap(): lax.ppermute(value, axis, [(i, i ^ key) for i in range(lax.axis_size(axis...  16 us
    pallas_call x1, Pallas kernels, forward(): pl.pallas_call(functools.partial(forward_kernel, peers, slots, crops, fra...  10.6 us
    pallas_call x4, Pallas kernels, kernel_call(): pl.pallas_call(kernel, in_specs=[SMEM_SPEC] + [VMEM_SPEC] * len(arrays),...  8.26 us
    unnamed x36, local copies, waits for them, and re-layouts  7.47 us
    pallas_call x1, Pallas kernels, backward(): pl.pallas_call(functools.partial(backward_kernel, crops, frames, channels...  5.75 us
    scatter x2, local copies, waits for them, and re-layouts, on_device(): taps.at[0:10, :channels].set(conv_first).at[5:15, channels:].set(conv_first)  2.53 us
  transfers between devices with their start and end apart: 14, of which 12 were waited for; matrix products, arithmetic and copies ran while one was open for 4% of the time, Pallas kernels for 8%

profile of v1, /device:TPU:0, one launch (start us, length us, event | category | flops | bytes accessed | tf_op | source)
XLA Modules:
  0.0 69.2 jit_solution(15107051333500806739)
XLA Ops:
  2.1 3.9 %collective-permute-start.2 = (bf16[8,2688]{1,0:T(8,128)(2,1)S(1)}, bf16[8,2688]{1,0:T(8,128)(2,1)S(1)}, u32[]{:S(2)}, u32[]{:S(2)}) collective-permute-start(bf16[8,2688]{1,0:T(8,128)(2,1)S(1)} %fusion.refs_0_), channel_id=1, source_target_pairs={{0,24},{8,16},{16,8},{24,0},{1,25},{9,17},{17,9},{25,1},{2,26},{10... | collective-permute-start | bytes 129032 | tf_op jit(solution)/shard_map/ppermute | solution.py:362
  7.5 1.8 %scatter.9.refs_5_.taps = bf16[128,1024]{1,0:T(8,128)(2,1)S(1)} dynamic-update-slice(bf16[128,1024]{1,0:T(8,128)(2,1)S(1)} %scatter.6, bf16[10,512]{1,0:T(8,128)(2,1)} %param.14, s32[]{:T(128)} %constant.88.clone.1, s32[]{:T(128)} %constant.89.clone.1) | dynamic-update-slice | bytes 20484 | tf_op jit(solution)/shard_map/scatter | solution.py:538
  10.5 1.4 %copy-done = bf16[1536,512]{1,0:T(8,128)(2,1)S(1)} copy-done((bf16[1536,512]{1,0:T(8,128)(2,1)S(1)}, bf16[1536,512]{1,0:T(8,128)(2,1)}, u32[]{:S(2)}) %copy-start) | copy-done | bytes 1572888
  11.9 1.2 %copy-done.3 = bf16[1,4,256,512]{3,2,1,0:T(8,128)(2,1)S(1)} copy-done((bf16[1,4,256,512]{3,2,1,0:T(8,128)(2,1)S(1)}, bf16[1,4,256,512]{3,2,1,0:T(8,128)(2,1)}, u32[]{:S(2)}) %copy-start.3) | copy-done | bytes 1048600
  14.5 10.6 %forward.1 = (f32[768,512]{1,0:T(8,128)S(1)}, bf16[768,512]{1,0:T(8,128)(2,1)S(1)}, bf16[4,256,512]{2,1,0:T(8,128)(2,1)S(1)}, bf16[4,264,128]{2,1,0:T(8,128)(2,1)S(1)}, f32[4,8,512]{2,1,0:T(8,128)S(1)}) custom-call(s32[3]{0:T(128)S(1)} %pad_add_fusion.where, bf16[8,2688]{1,0:T(8,128)(2,1)S(1)} %fusion.refs_0_, ...), custom_call_target="tpu_custom_call" | custom-call | tf_op jit(solution)/shard_map/forward/pallas_call | solution.py:179
  25.2 1.2 %copy-done.2 = f32[768,512]{1,0:T(8,128)} copy-done((f32[768,512]{1,0:T(8,128)}, f32[768,512]{1,0:T(8,128)S(1)}, u32[]{:S(2)}) %copy-start.2) | copy-done | bytes 1572888
  26.3 2.3 %collective-permute-done.3.received = bf16[768,512]{1,0:T(8,128)(2,1)S(1)} collective-permute-done((bf16[768,512]{1,0:T(8,128)(2,1)S(1)}, bf16[768,512]{1,0:T(8,128)(2,1)S(1)}, u32[]{:S(2)}, u32[]{:S(2)}) %collective-permute-start.3) | collective-permute-done | bytes 786464 | tf_op jit(solution)/shard_map/ppermute | solution.py:362
  29.5 2.7 %split_dx.1 = (f32[192,512]{1,0:T(8,128)}, bf16[192,512]{1,0:T(8,128)(2,1)}, bf16[192,512]{1,0:T(8,128)(2,1)}, bf16[192,512]{1,0:T(8,128)(2,1)}) custom-call(s32[3]{0:T(128)} %copy-done.5, f32[768,512]{1,0:T(8,128)} %copy-done.2, bf16[768,512]{1,0:T(8,128)(2,1)} %copy-done.10), custom_call_target="tpu_custom_call" | custom-call | tf_op jit(solution)/shard_map/split_dx/pallas_call | solution.py:372
  32.8 1.5 %collective-permute-start.6 = (bf16[192,512]{1,0:T(8,128)(2,1)}, bf16[192,512]{1,0:T(8,128)(2,1)}, u32[]{:S(2)}, u32[]{:S(2)}) collective-permute-start(bf16[192,512]{1,0:T(8,128)(2,1)} %get-tuple-element.47), channel_id=1, source_target_pairs={{0,16},{8,24},{16,0},{24,8},{1,17},{9,25},{17,1},{25,9},{2,18},{10... | collective-permute-start | bytes 589832 | tf_op jit(solution)/shard_map/ppermute | solution.py:362
  34.4 1.3 %collective-permute-start.7 = (bf16[192,512]{1,0:T(8,128)(2,1)}, bf16[192,512]{1,0:T(8,128)(2,1)}, u32[]{:S(2)}, u32[]{:S(2)}) collective-permute-start(bf16[192,512]{1,0:T(8,128)(2,1)} %get-tuple-element.48), channel_id=1, source_target_pairs={{0,24},{8,16},{16,8},{24,0},{1,25},{9,17},{17,9},{25,1},{2,26},{10... | collective-permute-start | bytes 589832 | tf_op jit(solution)/shard_map/ppermute | solution.py:362
  35.7 5.7 %backward.1.small = f32[16,512]{1,0:T(8,128)S(1)} custom-call(bf16[4,256,512]{2,1,0:T(8,128)(2,1)S(1)} %get-tuple-element.43.grad_rows, bf16[4,264,128]{2,1,0:T(8,128)(2,1)S(1)} %get-tuple-element.44.patches, f32[4,8,512]{2,1,0:T(8,128)S(1)} %get-tuple-element.45.stats, bf16[128,1024]{1,0:T(8,128)(2,1)S(1)} %scatter.9.refs_5_.taps, ...), custom_call_target="tpu_custom_call" | custom-call | tf_op jit(solution)/shard_map/backward/pallas_call | solution.py:326
  41.5 1.2 %collective-permute-done.4.small_received = f32[16,512]{1,0:T(8,128)S(1)} collective-permute-done((f32[16,512]{1,0:T(8,128)S(1)}, f32[16,512]{1,0:T(8,128)S(1)}, u32[]{:S(2)}, u32[]{:S(2)}) %collective-permute-start.4) | collective-permute-done | bytes 32800 | tf_op jit(solution)/shard_map/ppermute | solution.py:362
  43.1 1.5 %collective-permute-done.7.refs_2_ = bf16[192,512]{1,0:T(8,128)(2,1)} collective-permute-done((bf16[192,512]{1,0:T(8,128)(2,1)}, bf16[192,512]{1,0:T(8,128)(2,1)}, u32[]{:S(2)}, u32[]{:S(2)}) %collective-permute-start.7) | collective-permute-done | bytes 196640 | tf_op jit(solution)/shard_map/ppermute | solution.py:362
  44.6 2.1 %split_dy.1 = (f32[80,512]{1,0:T(8,128)}, bf16[80,512]{1,0:T(8,128)(2,1)}, bf16[80,512]{1,0:T(8,128)(2,1)}, bf16[80,512]{1,0:T(8,128)(2,1)}) custom-call(s32[3]{0:T(128)} %copy-done.5, f32[192,512]{1,0:T(8,128)} %get-tuple-element.42.own, f32[16,512]{1,0:T(8,128)} %copy-done.4, f32[16,512]{1,0:T(8,128)} %copy-done.17, ...), custom_call_target="tpu_custom_call" | custom-call | tf_op jit(solution)/shard_map/split_dy/pallas_call | solution.py:372
  46.7 1.6 %collective-permute-start.8 = (bf16[80,512]{1,0:T(8,128)(2,1)}, bf16[80,512]{1,0:T(8,128)(2,1)S(1)}, u32[]{:S(2)}, u32[]{:S(2)}) collective-permute-start(bf16[80,512]{1,0:T(8,128)(2,1)} %get-tuple-element.50), channel_id=1, source_target_pairs={{0,2},{1,3},{2,0},{3,1},{4,6},{5,7},{6,4},{7,5},{8,10},{9,11},{10,... | collective-permute-start | bytes 245768 | tf_op jit(solution)/shard_map/ppermute | solution.py:362
  48.3 2.6 %collective-permute-start.9 = (bf16[80,512]{1,0:T(8,128)(2,1)}, bf16[80,512]{1,0:T(8,128)(2,1)S(1)}, u32[]{:S(2)}, u32[]{:S(2)}) collective-permute-start(bf16[80,512]{1,0:T(8,128)(2,1)} %get-tuple-element.51), channel_id=1, source_target_pairs={{0,4},{1,5},{2,6},{3,7},{4,0},{5,1},{6,2},{7,3},{8,12},{9,13},{10,... | collective-permute-start | bytes 245768 | tf_op jit(solution)/shard_map/ppermute | solution.py:362
  51.1 1.1 %collective-permute-done.8.refs_0_ = bf16[80,512]{1,0:T(8,128)(2,1)S(1)} collective-permute-done((bf16[80,512]{1,0:T(8,128)(2,1)}, bf16[80,512]{1,0:T(8,128)(2,1)S(1)}, u32[]{:S(2)}, u32[]{:S(2)}) %collective-permute-start.8) | collective-permute-done | bytes 81952 | tf_op jit(solution)/shard_map/ppermute | solution.py:362
  52.2 4.1 %collective-permute-done.9.refs_1_ = bf16[80,512]{1,0:T(8,128)(2,1)S(1)} collective-permute-done((bf16[80,512]{1,0:T(8,128)(2,1)}, bf16[80,512]{1,0:T(8,128)(2,1)S(1)}, u32[]{:S(2)}, u32[]{:S(2)}) %collective-permute-start.9) | collective-permute-done | bytes 81952 | tf_op jit(solution)/shard_map/ppermute | solution.py:362
  56.2 1.2 %collective-permute-done.10.refs_2_ = bf16[80,512]{1,0:T(8,128)(2,1)S(1)} collective-permute-done((bf16[80,512]{1,0:T(8,128)(2,1)}, bf16[80,512]{1,0:T(8,128)(2,1)S(1)}, u32[]{:S(2)}, u32[]{:S(2)}) %collective-permute-start.10) | collective-permute-done | bytes 81952 | tf_op jit(solution)/shard_map/ppermute | solution.py:362
  58.0 1.7 %add_dy.1.refs_0_ = bf16[80,512]{1,0:T(8,128)(2,1)} custom-call(s32[3]{0:T(128)} %copy-done.5, f32[80,512]{1,0:T(8,128)} %get-tuple-element.49.own, bf16[80,512]{1,0:T(8,128)(2,1)} %copy-done.14, bf16[80,512]{1,0:T(8,128)(2,1)} %copy-done.15, bf16[80,512]{1,0:T(8,128)(2,1)} %copy-done.16), custom_call_target="tpu_custom_call" | custom-call | tf_op jit(solution)/shard_map/add_dy/pallas_call | solution.py:372
  59.7 1.8 %collective-permute-start.13 = (bf16[80,512]{1,0:T(8,128)(2,1)}, bf16[80,512]{1,0:T(8,128)(2,1)S(1)}, u32[]{:S(2)}, u32[]{:S(2)}) collective-permute-start(bf16[80,512]{1,0:T(8,128)(2,1)} %add_dy.1.refs_0_), channel_id=1, source_target_pairs={{0,24},{8,16},{16,8},{24,0},{1,25},{9,17},{17,9},{25,1},{2,26},{10... | collective-permute-start | bytes 245768 | tf_op jit(solution)/shard_map/ppermute | solution.py:362
  62.0 1.2 %collective-permute-start.11 = (bf16[80,512]{1,0:T(8,128)(2,1)}, bf16[80,512]{1,0:T(8,128)(2,1)S(1)}, u32[]{:S(2)}, u32[]{:S(2)}) collective-permute-start(bf16[80,512]{1,0:T(8,128)(2,1)} %add_dy.1.refs_0_), channel_id=1, source_target_pairs={{0,8},{8,0},{16,24},{24,16},{1,9},{9,1},{17,25},{25,17},{2,10},{10... | collective-permute-start | bytes 245768 | tf_op jit(solution)/shard_map/ppermute | solution.py:362
  63.2 2.1 %collective-permute-done.13.refs_3_ = bf16[80,512]{1,0:T(8,128)(2,1)S(1)} collective-permute-done((bf16[80,512]{1,0:T(8,128)(2,1)}, bf16[80,512]{1,0:T(8,128)(2,1)S(1)}, u32[]{:S(2)}, u32[]{:S(2)}) %collective-permute-start.13) | collective-permute-done | bytes 81952 | tf_op jit(solution)/shard_map/ppermute | solution.py:362
  67.4 1.8 %assemble.1 = (f32[10,512]{1,0:T(8,128)}, f32[2,512]{1,0:T(2,128)}, f32[192,512]{1,0:T(8,128)}) custom-call(s32[3]{0:T(128)} %copy-done.5, bf16[80,512]{1,0:T(8,128)(2,1)} %add_dy.1.refs_0_, bf16[80,512]{1,0:T(8,128)(2,1)} %copy-done.13, bf16[80,512]{1,0:T(8,128)(2,1)} %copy-done.12, bf16[80,512]{1,0:T(8,128)(2,1)} %copy-done.11), custom_call_target="tpu_custom_call" | custom-call | tf_op jit(solution)/shard_map/assemble/pallas_call | solution.py:372
  (50 shorter events, 10.4 us)
Async XLA Ops:
  2.1 7.2 %collective-permute-start.2 = (bf16[8,2688]{1,0:T(8,128)(2,1)S(1)}, bf16[8,2688]{1,0:T(8,128)(2,1)S(1)}, u32[]{:S(2)}, u32[]{:S(2)}) collective-permute-start(bf16[8,2688]{1,0:T(8,128)(2,1)S(1)} %fusion.refs_0_), channel_id=1, source_target_pairs={{0,24},{8,16},{16,8},{24,0},{1,25},{9,17},{17,9},{25,1},{2,26},{10... | collective-permute-start | bytes 129032 | tf_op jit(solution)/shard_map/ppermute | solution.py:362
  6.0 4.0 %collective-permute-start.1 = (bf16[8,2688]{1,0:T(8,128)(2,1)S(1)}, bf16[8,2688]{1,0:T(8,128)(2,1)S(1)}, u32[]{:S(2)}, u32[]{:S(2)}) collective-permute-start(bf16[8,2688]{1,0:T(8,128)(2,1)S(1)} %fusion.refs_0_), channel_id=1, source_target_pairs={{0,16},{8,24},{16,0},{24,8},{1,17},{9,25},{17,1},{25,9},{2,18},{10... | collective-permute-start | bytes 129032 | tf_op jit(solution)/shard_map/ppermute | solution.py:362
  6.5 4.0 %collective-permute-start = (bf16[8,2688]{1,0:T(8,128)(2,1)S(1)}, bf16[8,2688]{1,0:T(8,128)(2,1)S(1)}, u32[]{:S(2)}, u32[]{:S(2)}) collective-permute-start(bf16[8,2688]{1,0:T(8,128)(2,1)S(1)} %fusion.refs_0_), channel_id=1, source_target_pairs={{0,8},{8,0},{16,24},{24,16},{1,9},{9,1},{17,25},{25,17},{2,10},{10... | collective-permute-start | bytes 129032 | tf_op jit(solution)/shard_map/ppermute | solution.py:362
  6.7 18.4 %copy-start.5 = (s32[3]{0:T(128)}, s32[3]{0:T(128)S(1)}, u32[]{:S(2)}) copy-start(s32[3]{0:T(128)S(1)} %pad_add_fusion.where) | copy-start | bytes 40
  10.5 1.4 %copy-start = (bf16[1536,512]{1,0:T(8,128)(2,1)S(1)}, bf16[1536,512]{1,0:T(8,128)(2,1)}, u32[]{:S(2)}) copy-start(bf16[1536,512]{1,0:T(8,128)(2,1)} %second.1) | copy-start | bytes 4718596
  11.9 1.2 %copy-start.3 = (bf16[1,4,256,512]{3,2,1,0:T(8,128)(2,1)S(1)}, bf16[1,4,256,512]{3,2,1,0:T(8,128)(2,1)}, u32[]{:S(2)}) copy-start(bf16[1,4,256,512]{3,2,1,0:T(8,128)(2,1)} %param.13) | copy-start | bytes 3145732
  26.3 9.4 %copy-start.1 = (bf16[1536,512]{1,0:T(8,128)(2,1)S(1)}, bf16[1536,512]{1,0:T(8,128)(2,1)}, u32[]{:S(2)}) copy-start(bf16[1536,512]{1,0:T(8,128)(2,1)} %second.1) | copy-start | bytes 4718596
  26.3 9.4 %copy-start.7 = (f32[512]{0:T(512)S(1)}, f32[512]{0:T(512)}, u32[]{:S(2)}) copy-start(f32[512]{0:T(512)} %param.15) | copy-start | bytes 6148
  26.3 9.4 %copy-start.9 = (f32[512]{0:T(512)S(1)}, f32[512]{0:T(512)}, u32[]{:S(2)}) copy-start(f32[512]{0:T(512)} %param.16) | copy-start | bytes 6148
  26.3 2.3 %collective-permute-start.3 = (bf16[768,512]{1,0:T(8,128)(2,1)S(1)}, bf16[768,512]{1,0:T(8,128)(2,1)S(1)}, u32[]{:S(2)}, u32[]{:S(2)}) collective-permute-start(bf16[768,512]{1,0:T(8,128)(2,1)S(1)} %get-tuple-element.41), channel_id=1, source_target_pairs={{0,1},{1,0},{2,3},{3,2},{4,5},{5,4},{6,7},{7,6},{8,9},{9,8},{10,11... | collective-permute-start | bytes 2359304 | tf_op jit(solution)/shard_map/ppermute | solution.py:362
  32.2 10.5 %collective-permute-start.5 = (bf16[192,512]{1,0:T(8,128)(2,1)}, bf16[192,512]{1,0:T(8,128)(2,1)}, u32[]{:S(2)}, u32[]{:S(2)}) collective-permute-start(bf16[192,512]{1,0:T(8,128)(2,1)} %get-tuple-element.46), channel_id=1, source_target_pairs={{0,8},{8,0},{16,24},{24,16},{1,9},{9,1},{17,25},{25,17},{2,10},{10... | collective-permute-start | bytes 589832 | tf_op jit(solution)/shard_map/ppermute | solution.py:362
  32.8 10.3 %collective-permute-start.6 = (bf16[192,512]{1,0:T(8,128)(2,1)}, bf16[192,512]{1,0:T(8,128)(2,1)}, u32[]{:S(2)}, u32[]{:S(2)}) collective-permute-start(bf16[192,512]{1,0:T(8,128)(2,1)} %get-tuple-element.47), channel_id=1, source_target_pairs={{0,16},{8,24},{16,0},{24,8},{1,17},{9,25},{17,1},{25,9},{2,18},{10... | collective-permute-start | bytes 589832 | tf_op jit(solution)/shard_map/ppermute | solution.py:362
  34.4 10.3 %collective-permute-start.7 = (bf16[192,512]{1,0:T(8,128)(2,1)}, bf16[192,512]{1,0:T(8,128)(2,1)}, u32[]{:S(2)}, u32[]{:S(2)}) collective-permute-start(bf16[192,512]{1,0:T(8,128)(2,1)} %get-tuple-element.48), channel_id=1, source_target_pairs={{0,24},{8,16},{16,8},{24,0},{1,25},{9,17},{17,9},{25,1},{2,26},{10... | collective-permute-start | bytes 589832 | tf_op jit(solution)/shard_map/ppermute | solution.py:362
  41.4 3.2 %copy-start.4 = (f32[16,512]{1,0:T(8,128)}, f32[16,512]{1,0:T(8,128)S(1)}, u32[]{:S(2)}) copy-start(f32[16,512]{1,0:T(8,128)S(1)} %backward.1.small) | copy-start | bytes 98308
  41.5 1.3 %collective-permute-start.4 = (f32[16,512]{1,0:T(8,128)S(1)}, f32[16,512]{1,0:T(8,128)S(1)}, u32[]{:S(2)}, u32[]{:S(2)}) collective-permute-start(f32[16,512]{1,0:T(8,128)S(1)} %backward.1.small), channel_id=1, source_target_pairs={{0,1},{1,0},{2,3},{3,2},{4,5},{5,4},{6,7},{7,6},{8,9},{9,8},{10,11... | collective-permute-start | bytes 98312 | tf_op jit(solution)/shard_map/ppermute | solution.py:362
  42.7 1.9 %copy-start.17 = (f32[16,512]{1,0:T(8,128)}, f32[16,512]{1,0:T(8,128)S(1)}, u32[]{:S(2)}) copy-start(f32[16,512]{1,0:T(8,128)S(1)} %collective-permute-done.4.small_received) | copy-start | bytes 98308
  46.7 5.5 %collective-permute-start.8 = (bf16[80,512]{1,0:T(8,128)(2,1)}, bf16[80,512]{1,0:T(8,128)(2,1)S(1)}, u32[]{:S(2)}, u32[]{:S(2)}) collective-permute-start(bf16[80,512]{1,0:T(8,128)(2,1)} %get-tuple-element.50), channel_id=1, source_target_pairs={{0,2},{1,3},{2,0},{3,1},{4,6},{5,7},{6,4},{7,5},{8,10},{9,11},{10,... | collective-permute-start | bytes 245768 | tf_op jit(solution)/shard_map/ppermute | solution.py:362
  48.3 8.0 %collective-permute-start.9 = (bf16[80,512]{1,0:T(8,128)(2,1)}, bf16[80,512]{1,0:T(8,128)(2,1)S(1)}, u32[]{:S(2)}, u32[]{:S(2)}) collective-permute-start(bf16[80,512]{1,0:T(8,128)(2,1)} %get-tuple-element.51), channel_id=1, source_target_pairs={{0,4},{1,5},{2,6},{3,7},{4,0},{5,1},{6,2},{7,3},{8,12},{9,13},{10,... | collective-permute-start | bytes 245768 | tf_op jit(solution)/shard_map/ppermute | solution.py:362
  50.8 6.5 %collective-permute-start.10 = (bf16[80,512]{1,0:T(8,128)(2,1)}, bf16[80,512]{1,0:T(8,128)(2,1)S(1)}, u32[]{:S(2)}, u32[]{:S(2)}) collective-permute-start(bf16[80,512]{1,0:T(8,128)(2,1)} %get-tuple-element.52), channel_id=1, source_target_pairs={{0,6},{1,7},{2,4},{3,5},{4,2},{5,3},{6,0},{7,1},{8,14},{9,15},{10,... | collective-permute-start | bytes 245768 | tf_op jit(solution)/shard_map/ppermute | solution.py:362
  52.2 5.2 %copy-start.14 = (bf16[80,512]{1,0:T(8,128)(2,1)}, bf16[80,512]{1,0:T(8,128)(2,1)S(1)}, u32[]{:S(2)}) copy-start(bf16[80,512]{1,0:T(8,128)(2,1)S(1)} %collective-permute-done.8.refs_0_) | copy-start | bytes 245764
  59.7 5.6 %collective-permute-start.13 = (bf16[80,512]{1,0:T(8,128)(2,1)}, bf16[80,512]{1,0:T(8,128)(2,1)S(1)}, u32[]{:S(2)}, u32[]{:S(2)}) collective-permute-start(bf16[80,512]{1,0:T(8,128)(2,1)} %add_dy.1.refs_0_), channel_id=1, source_target_pairs={{0,24},{8,16},{16,8},{24,0},{1,25},{9,17},{17,9},{25,1},{2,26},{10... | collective-permute-start | bytes 245768 | tf_op jit(solution)/shard_map/ppermute | solution.py:362
  61.5 4.7 %collective-permute-start.12 = (bf16[80,512]{1,0:T(8,128)(2,1)}, bf16[80,512]{1,0:T(8,128)(2,1)S(1)}, u32[]{:S(2)}, u32[]{:S(2)}) collective-permute-start(bf16[80,512]{1,0:T(8,128)(2,1)} %add_dy.1.refs_0_), channel_id=1, source_target_pairs={{0,16},{8,24},{16,0},{24,8},{1,17},{9,25},{17,1},{25,9},{2,18},{10... | collective-permute-start | bytes 245768 | tf_op jit(solution)/shard_map/ppermute | solution.py:362
  62.0 4.7 %collective-permute-start.11 = (bf16[80,512]{1,0:T(8,128)(2,1)}, bf16[80,512]{1,0:T(8,128)(2,1)S(1)}, u32[]{:S(2)}, u32[]{:S(2)}) collective-permute-start(bf16[80,512]{1,0:T(8,128)(2,1)} %add_dy.1.refs_0_), channel_id=1, source_target_pairs={{0,8},{8,0},{16,24},{24,16},{1,9},{9,1},{17,25},{25,17},{2,10},{10... | collective-permute-start | bytes 245768 | tf_op jit(solution)/shard_map/ppermute | solution.py:362
  65.3 1.4 %copy-start.11 = (bf16[80,512]{1,0:T(8,128)(2,1)}, bf16[80,512]{1,0:T(8,128)(2,1)S(1)}, u32[]{:S(2)}) copy-start(bf16[80,512]{1,0:T(8,128)(2,1)S(1)} %collective-permute-done.13.refs_3_) | copy-start | bytes 245764
  (8 other events, 6.5 us)
